TPU v7x, 32 devices: a whole 2x2x4 slice. The times are simulated.
32 devices in a mesh: rep: 8 (over y, x, core), shard: 4 (over z).
Axes of the slice: x: 2, y: 2, z: 4, core: 2. Of those that a mesh axis runs over, the one named last changes fastest.
Arguments:
- layer_input: bfloat16 [16384, 768], P(('rep', 'shard')), may hold values from -6 to 6
- query_weight: bfloat16 [768, 768], P('shard'), may hold values from -0.21875 to 0.21875
- key_weight: bfloat16 [768, 768], P('shard'), may hold values from -0.21875 to 0.21875
- value_weight: bfloat16 [768, 768], P('shard'), may hold values from -0.21875 to 0.21875
- output_weight: bfloat16 [768, 768], P('shard'), may hold values from -6 to 6
- inner_weight: bfloat16 [768, 3072], P('shard'), may hold values from -0.21875 to 0.21875
- outer_weight: bfloat16 [3072, 768], P('shard'), may hold values from -0.109375 to 0.109375
- query_bias: float32 [768], replicated, may hold values from -3 to 3
- value_bias: float32 [768], replicated, may hold values from -3 to 3
- output_bias: float32 [768], replicated, may hold values from -3 to 3
- inner_bias: float32 [3072], replicated, may hold values from -3 to 3
- outer_bias: float32 [768], replicated, may hold values from -3 to 3
- attn_gain: float32 [768], replicated, may hold values from 0.25 to 1.75
- attn_shift: float32 [768], replicated, may hold values from -3 to 3
- ffn_gain: float32 [768], replicated, may hold values from 0.25 to 1.75
- ffn_shift: float32 [768], replicated, may hold values from -3 to 3
- cotangent: bfloat16 [16384, 768], P(('rep', 'shard')), may hold values from -6 to 6
Outputs:
- layer_output: bfloat16 [16384, 768], P(('rep', 'shard'))
- input_grad: float32 [16384, 768], P(('rep', 'shard'))
- grad_query_weight: float32 [768, 768], P('shard')
- grad_key_weight: float32 [768, 768], P('shard')
- grad_value_weight: float32 [768, 768], P('shard')
- grad_output_weight: float32 [768, 768], P('shard')
- grad_inner_weight: float32 [768, 3072], P('shard')
- grad_outer_weight: float32 [3072, 768], P('shard')
- grad_query_bias: float32 [768], replicated
- grad_value_bias: float32 [768], replicated
- grad_output_bias: float32 [768], replicated
- grad_inner_bias: float32 [3072], replicated
- grad_outer_bias: float32 [768], replicated
- grad_attn_gain: float32 [768], replicated
- grad_attn_shift: float32 [768], replicated
- grad_ffn_gain: float32 [768], replicated
- grad_ffn_shift: float32 [768], replicated
All inputs are finite; a program needn't handle non-finite values.
Results may differ from a plain program's by a relative error of at most 0.02.
Values may be sent and summed in bfloat16 or wider, within the bound.
A program may use at most 128 MiB of HBM per device.

v0:
```python
from functools import partial

import jax
import jax.numpy as jnp
from jax import lax
from jax.sharding import PartitionSpec as P

HEADS = 12
HD = 64


eps_norm = 1e-05


def layer_norm(values, norm_gain, norm_shift):
    row_mean = jnp.mean(values, axis=-1, keepdims=True)
    centered = values - row_mean
    variance = jnp.mean(centered * centered, axis=-1, keepdims=True)
    return centered * lax.rsqrt(variance + eps_norm) * norm_gain + norm_shift


def project(left, right):
    return jnp.dot(left, right, preferred_element_type=jnp.float32)


def project_back(left, right):
    return lax.dot_general(
        left, right, (((1,), (1,)), ((), ())), preferred_element_type=jnp.float32
    )


def outer_sum(left, right):
    return lax.dot_general(
        left, right, (((0,), (0,)), ((), ())), preferred_element_type=jnp.float32
    )


def to_pairs(matrix):
    return matrix.reshape(matrix.shape[0], HEADS // 2, 2 * HD).transpose(1, 0, 2)


def from_pairs(stacked):
    return stacked.transpose(1, 0, 2).reshape(stacked.shape[1], HEADS * HD)


def split_heads(pair):
    return pair.reshape(pair.shape[0], 2, HD)


def attend_pair(operands):
    query_pair, key_pair, value_pair = operands
    scale = HD ** (-0.5)
    scores = (
        jnp.einsum(
            "qhd,khd->hqk",
            split_heads(query_pair),
            split_heads(key_pair),
            preferred_element_type=jnp.float32,
        )
        * scale
    )
    row_max = jnp.max(scores, axis=-1, keepdims=True)
    exp_scores = jnp.exp(scores - row_max)
    exp_total = jnp.sum(exp_scores, axis=-1, keepdims=True)
    attn_probs = (exp_scores / exp_total).astype(jnp.bfloat16)
    context = jnp.einsum(
        "hqk,khd->qhd", attn_probs, split_heads(value_pair), preferred_element_type=jnp.float32
    )
    log_total = (row_max + jnp.log(exp_total))[..., 0]
    return (context.reshape(context.shape[0], 2 * HD), log_total)


def attend_back(operands):
    query_pair, key_pair, value_pair, grad_pair, log_total = operands
    scale = HD ** (-0.5)
    query_heads = split_heads(query_pair)
    key_heads = split_heads(key_pair)
    value_heads = split_heads(value_pair)
    grad_heads = split_heads(grad_pair)
    scores = (
        jnp.einsum("qhd,khd->hqk", query_heads, key_heads, preferred_element_type=jnp.float32)
        * scale
    )
    attn_probs = jnp.exp(scores - log_total[..., None])
    grad_probs = jnp.einsum(
        "qhd,khd->hqk", grad_heads, value_heads, preferred_element_type=jnp.float32
    )
    row_dot = jnp.sum(attn_probs * grad_probs, axis=-1, keepdims=True)
    grad_scores = (attn_probs * (grad_probs - row_dot) * scale).astype(jnp.bfloat16)
    grad_query = jnp.einsum(
        "hqk,khd->qhd", grad_scores, key_heads, preferred_element_type=jnp.float32
    )
    grad_key = jnp.einsum(
        "hqk,qhd->khd", grad_scores, query_heads, preferred_element_type=jnp.float32
    )
    grad_value = jnp.einsum(
        "hqk,qhd->khd",
        attn_probs.astype(jnp.bfloat16),
        grad_heads,
        preferred_element_type=jnp.float32,
    )
    length = query_pair.shape[0]
    return tuple(
        (
            member.reshape(length, 2 * HD).astype(jnp.bfloat16)
            for member in (grad_query, grad_key, grad_value)
        )
    )


def forward(tokens, weights, small):
    query_weight, key_weight, value_weight, output_weight, inner_weight, outer_weight = weights
    (
        query_bias,
        value_bias,
        output_bias,
        inner_bias,
        outer_bias,
        attn_gain,
        attn_shift,
        ffn_gain,
        ffn_shift,
    ) = small
    query_rows = (project(tokens, query_weight) + query_bias).astype(jnp.bfloat16)
    key_rows = project(tokens, key_weight).astype(jnp.bfloat16)
    value_rows = (project(tokens, value_weight) + value_bias).astype(jnp.bfloat16)
    contexts, log_totals = lax.map(
        attend_pair, (to_pairs(query_rows), to_pairs(key_rows), to_pairs(value_rows))
    )
    context = from_pairs(contexts).astype(jnp.bfloat16)
    residual_one = tokens.astype(jnp.float32) + project(context, output_weight) + output_bias
    first_norm = layer_norm(residual_one, attn_gain, attn_shift)
    first_low = first_norm.astype(jnp.bfloat16)
    pre_act = project(first_low, inner_weight) + inner_bias
    hidden = jax.nn.gelu(pre_act, approximate=False).astype(jnp.bfloat16)
    residual_two = first_norm + project(hidden, outer_weight) + outer_bias
    result = layer_norm(residual_two, ffn_gain, ffn_shift)
    state = (
        query_rows,
        key_rows,
        value_rows,
        log_totals,
        context,
        residual_one,
        first_low,
        pre_act,
        hidden,
        residual_two,
    )
    return (result, state)


def backward(tokens, weights, small, cotangent):
    query_weight, key_weight, value_weight, output_weight, inner_weight, outer_weight = weights
    (
        query_bias,
        value_bias,
        output_bias,
        inner_bias,
        outer_bias,
        attn_gain,
        attn_shift,
        ffn_gain,
        ffn_shift,
    ) = small
    unused, state = forward(tokens, weights, small)
    (
        query_rows,
        key_rows,
        value_rows,
        log_totals,
        context,
        residual_one,
        first_low,
        pre_act,
        hidden,
        residual_two,
    ) = state
    unused_two, norm_back = jax.vjp(layer_norm, residual_two, ffn_gain, ffn_shift)
    grad_two, grad_ffn_gain, grad_ffn_shift = norm_back(cotangent.astype(jnp.float32))
    grad_outer = grad_two.astype(jnp.bfloat16)
    grad_outer_weight = outer_sum(hidden, grad_outer)
    grad_outer_bias = jnp.sum(grad_outer, axis=0, dtype=jnp.float32)
    grad_hidden = project_back(grad_outer, outer_weight)
    unused_three, gelu_back = jax.vjp(partial(jax.nn.gelu, approximate=False), pre_act)
    grad_pre = gelu_back(grad_hidden)[0].astype(jnp.bfloat16)
    grad_inner_weight = outer_sum(first_low, grad_pre)
    grad_inner_bias = jnp.sum(grad_pre, axis=0, dtype=jnp.float32)
    grad_first = grad_two + project_back(grad_pre, inner_weight)
    unused_four, first_back = jax.vjp(layer_norm, residual_one, attn_gain, attn_shift)
    grad_one, grad_attn_gain, grad_attn_shift = first_back(grad_first)
    grad_mixed = grad_one.astype(jnp.bfloat16)
    grad_output_weight = outer_sum(context, grad_mixed)
    grad_output_bias = jnp.sum(grad_mixed, axis=0, dtype=jnp.float32)
    grad_context = project_back(grad_mixed, output_weight).astype(jnp.bfloat16)
    query_pairs, key_pairs, value_pairs = lax.map(
        attend_back,
        (
            to_pairs(query_rows),
            to_pairs(key_rows),
            to_pairs(value_rows),
            to_pairs(grad_context),
            log_totals,
        ),
    )
    grad_query = from_pairs(query_pairs)
    grad_keys = from_pairs(key_pairs)
    grad_values = from_pairs(value_pairs)
    grad_query_weight = outer_sum(tokens, grad_query)
    grad_key_weight = outer_sum(tokens, grad_keys)
    grad_value_weight = outer_sum(tokens, grad_values)
    grad_query_bias = jnp.sum(grad_query, axis=0, dtype=jnp.float32)
    grad_value_bias = jnp.sum(grad_values, axis=0, dtype=jnp.float32)
    input_grad = (
        grad_one
        + project_back(grad_query, query_weight)
        + project_back(grad_keys, key_weight)
        + project_back(grad_values, value_weight)
    )
    grad_mats = (
        grad_query_weight,
        grad_key_weight,
        grad_value_weight,
        grad_output_weight,
        grad_inner_weight,
        grad_outer_weight,
    )
    grad_small = (
        grad_query_bias,
        grad_value_bias,
        grad_output_bias,
        grad_inner_bias,
        grad_outer_bias,
        grad_attn_gain,
        grad_attn_shift,
        grad_ffn_gain,
        grad_ffn_shift,
    )
    return (input_grad, grad_mats, grad_small)


def shards(
    layer_input,
    query_weight,
    key_weight,
    value_weight,
    output_weight,
    inner_weight,
    outer_weight,
    query_bias,
    value_bias,
    output_bias,
    inner_bias,
    outer_bias,
    attn_gain,
    attn_shift,
    ffn_gain,
    ffn_shift,
    cotangent,
):
    small = (
        query_bias,
        value_bias,
        output_bias,
        inner_bias,
        outer_bias,
        attn_gain,
        attn_shift,
        ffn_gain,
        ffn_shift,
    )
    weights = (
        lax.all_gather(query_weight, "shard", axis=0, tiled=True),
        lax.all_gather(key_weight, "shard", axis=0, tiled=True),
        lax.all_gather(value_weight, "shard", axis=0, tiled=True),
        lax.all_gather(output_weight, "shard", axis=0, tiled=True),
        lax.all_gather(inner_weight, "shard", axis=0, tiled=True),
        lax.all_gather(outer_weight, "shard", axis=0, tiled=True),
    )
    result, unused = forward(layer_input, weights, small)
    layer_output = result.astype(jnp.bfloat16)
    weights_back = (
        lax.all_gather(query_weight, "shard", axis=0, tiled=True),
        lax.all_gather(key_weight, "shard", axis=0, tiled=True),
        lax.all_gather(value_weight, "shard", axis=0, tiled=True),
        lax.all_gather(output_weight, "shard", axis=0, tiled=True),
        lax.all_gather(inner_weight, "shard", axis=0, tiled=True),
        lax.all_gather(outer_weight, "shard", axis=0, tiled=True),
    )
    input_grad, grad_mats, grad_small = backward(layer_input, weights_back, small, cotangent)
    row_shards = (
        lax.psum_scatter(
            grad_mats[0].astype(jnp.bfloat16), "shard", scatter_dimension=0, tiled=True
        ).astype(jnp.float32),
        lax.psum_scatter(
            grad_mats[1].astype(jnp.bfloat16), "shard", scatter_dimension=0, tiled=True
        ).astype(jnp.float32),
        lax.psum_scatter(
            grad_mats[2].astype(jnp.bfloat16), "shard", scatter_dimension=0, tiled=True
        ).astype(jnp.float32),
        lax.psum_scatter(
            grad_mats[3].astype(jnp.bfloat16), "shard", scatter_dimension=0, tiled=True
        ).astype(jnp.float32),
        lax.psum_scatter(
            grad_mats[4].astype(jnp.bfloat16), "shard", scatter_dimension=0, tiled=True
        ).astype(jnp.float32),
        lax.psum_scatter(
            grad_mats[5].astype(jnp.bfloat16), "shard", scatter_dimension=0, tiled=True
        ).astype(jnp.float32),
    )
    summed_mats = (
        lax.psum(row_shards[0].astype(jnp.bfloat16), "rep").astype(jnp.float32),
        lax.psum(row_shards[1].astype(jnp.bfloat16), "rep").astype(jnp.float32),
        lax.psum(row_shards[2].astype(jnp.bfloat16), "rep").astype(jnp.float32),
        lax.psum(row_shards[3].astype(jnp.bfloat16), "rep").astype(jnp.float32),
        lax.psum(row_shards[4].astype(jnp.bfloat16), "rep").astype(jnp.float32),
        lax.psum(row_shards[5].astype(jnp.bfloat16), "rep").astype(jnp.float32),
    )
    summed_small = lax.psum(
        (
            grad_small[0],
            grad_small[1],
            grad_small[2],
            grad_small[3],
            grad_small[4],
            grad_small[5],
            grad_small[6],
            grad_small[7],
            grad_small[8],
        ),
        ("rep", "shard"),
    )
    return (
        layer_output,
        input_grad,
        summed_mats[0],
        summed_mats[1],
        summed_mats[2],
        summed_mats[3],
        summed_mats[4],
        summed_mats[5],
        summed_small[0],
        summed_small[1],
        summed_small[2],
        summed_small[3],
        summed_small[4],
        summed_small[5],
        summed_small[6],
        summed_small[7],
        summed_small[8],
    )


def solution(mesh):
    return jax.shard_map(
        shards,
        mesh=mesh,
        in_specs=(
            P(("rep", "shard"), None),
            P("shard", None),
            P("shard", None),
            P("shard", None),
            P("shard", None),
            P("shard", None),
            P("shard", None),
            P(),
            P(),
            P(),
            P(),
            P(),
            P(),
            P(),
            P(),
            P(),
            P(("rep", "shard"), None),
        ),
        out_specs=(
            P(("rep", "shard"), None),
            P(("rep", "shard"), None),
            P("shard", None),
            P("shard", None),
            P("shard", None),
            P("shard", None),
            P("shard", None),
            P("shard", None),
            P(),
            P(),
            P(),
            P(),
            P(),
            P(),
            P(),
            P(),
            P(),
        ),
        check_vma=False,
    )
```

profile of v0, /device:TPU:0, one launch (start us, length us, event | category | flops | bytes accessed | tf_op | source)
XLA Modules:
  0.0 844.2 jit_solution(8751087749379171377)
XLA Ops:
  11.3 31.5 %all-gather.7.cloned.1.call-done = bf16[768,768]{1,0:T(8,128)(2,1)} async-done(((bf16[192,768]{1,0:T(8,128)(2,1)}), bf16[768,768]{1,0:T(8,128)(2,1)}) %all-gather.7.cloned.1.call-update) | async-done | bytes 1179664 | tf_op jit(solution)/shard_map/all_gather | solution.py:275
  45.1 28.8 %all-gather.9.cloned.1.call-done = bf16[768,768]{1,0:T(8,128)(2,1)} async-done(((bf16[192,768]{1,0:T(8,128)(2,1)}), bf16[768,768]{1,0:T(8,128)(2,1)}) %all-gather.9.cloned.1.call-update) | async-done | bytes 1179664 | tf_op jit(solution)/shard_map/all_gather | solution.py:273
  76.3 28.8 %all-gather.11.cloned.1.call-done = bf16[768,768]{1,0:T(8,128)(2,1)} async-done(((bf16[192,768]{1,0:T(8,128)(2,1)}), bf16[768,768]{1,0:T(8,128)(2,1)}) %all-gather.11.cloned.1.call-update) | async-done | bytes 1179664 | tf_op jit(solution)/shard_map/all_gather | solution.py:274
  107.8 13.2 %while.37 = (s32[]{:T(128)}, bf16[6,512,128]{1,2,0:T(8,128)(2,1)S(1)}, f32[6,2,512]{2,1,0:T(2,128)}, bf16[6,512,128]{1,2,0:T(8,128)(2,1)S(1)}, bf16[6,512,128]{1...) while((s32[]{:T(128)}, bf16[6,512,128]{1,2,0:T(8,128)(2,1)S(1)}, ...), condition=%wide.region_11.12_spmd, body=%wide.region_8.11_spmd.sunk | while | flops 138935296 | bytes 7897689 | solution.py:127
  122.1 16.1 %while.36 = (s32[]{:T(128)}, bf16[6,512,128]{1,2,0:T(8,128)(2,1)}, bf16[6,512,128]{1,2,0:T(8,128)(2,1)S(1)}, bf16[6,512,128]{1,2,0:T(8,128)(2,1)S(1)}, bf16[6,512,128]{1,2,0:T(8,128)(2,1)S(1)}, /*index=5*/s32[]{:T(128)}) while((s32[]{:T(128)}, bf16[6,512,128]{1,2,0:T(8,128)(2,1)}, bf16[6,512,128]{1,2,0:T(8,128)(2,1)S(1)}, ...), condition=%wide.region_3.4_spmd, body=%wide.region_0.3_spmd.sunk | while | flops 204998656 | bytes 1843789 | solution.py:127
  138.3 3.2 fusion.117
  144.3 81.8 %all-gather.15.cloned.1.call-done = bf16[768,3072]{1,0:T(8,128)(2,1)} async-done(((bf16[192,3072]{1,0:T(8,128)(2,1)}), bf16[768,3072]{1,0:T(8,128)(2,1)}) %all-gather.15.cloned.1.call-update) | async-done | bytes 4718608 | tf_op jit(solution)/shard_map/all_gather | solution.py:277
  226.1 20.9 %multiply_convert_fusion.1 = (bf16[512,3072]{1,0:T(8,128)(2,1)}, f32[512,3072]{1,0:T(8,128)}, f32[512,3072]{1,0:T(8,128)}) fusion(f32[3072]{0:T(1024)S(1)} %copy-done.37, bf16[768,3072]{1,0:T(8,128)(2,1)} %all-gather.15.cloned.1.call-done, f32[512,768]{1,0:T(8,128)} %copy-done.4, f32[512]{0:T(512)S(1)} %fusion.78, f32[512]{0:T(512)S(1)} %broadcast_multiply_fusion.1, ...), kind=kOutput, calls=%fused_computation.59 | convolution fusion | flops 2521694208 | bytes 22042624 | tf_op jit(solution)/shard_map/dot_general | solution.py:23
  247.1 68.4 %all-gather.17.cloned.1.call-done = bf16[3072,768]{1,0:T(8,128)(2,1)} async-done(((bf16[768,768]{1,0:T(8,128)(2,1)}), bf16[3072,768]{1,0:T(8,128)(2,1)}) %all-gather.17.cloned.1.call-update) | async-done | bytes 4718608 | tf_op jit(solution)/shard_map/all_gather | solution.py:278
  315.4 6.5 fusion.118
  322.2 23.0 %fusion.120 = (f32[512]{0:T(512)S(1)}, f32[512,768]{1,0:T(8,128)}) fusion(f32[768]{0:T(1024)S(1)} %copy-done.41, bf16[3072,768]{1,0:T(8,128)(2,1)} %all-gather.17.cloned.1.call-done, bf16[768,3072]{1,0:T(8,128)(2,1)} %all-gather.15.cloned.1.call-done, f32[3072]{0:T(1024)S(1)} %copy-done.37, f32[512,768]{1,0:T(8,128)} %copy-done.10, ...), kind=kOutput, calls=%fused_computation.191 | convolution fusion | flops 4940365312 | bytes 12610560 | tf_op jit(solution)/shard_map/dot_general | solution.py:23
  350.4 8.6 %convert_reduce_fusion = (f32[3072]{0:T(1024)S(1)}, bf16[512,3072]{1,0:T(8,128)(2,1)S(1)}) fusion(f32[512,3072]{1,0:T(8,128)} %get-tuple-element.255, f32[512,3072]{1,0:T(8,128)} %get-tuple-element.267, f32[3072]{0:T(1024)S(1)} %copy-done.37, bf16[512,768]{1,0:T(8,128)(2,1)S(1)} %get-tuple-element.245, bf16[3072,768]{1,0:T(8,128)(2,1)S(1)} %copy-done.27), kind=kOutput, calls=%fused_computation.57 | convolution fusion | flops 2442654720 | bytes 21258240 | tf_op jit(solution)/shard_map/dot_general | solution.py:27
  359.2 3.2 multiply_reduce_fusion.3
  367.2 81.0 %while.38 = (s32[]{:T(128)}, bf16[6,512,128]{1,2,0:T(8,128)(2,1)}, bf16[6,512,128]{1,2,0:T(8,128)(2,1)}, bf16[6,512,128]{1,2,0:T(8,128)(2,1)}, bf16[6,512,128]{1...) while((s32[]{:T(128)}, bf16[6,512,128]{1,2,0:T(8,128)(2,1)}, ...), condition=%wide.region_22.23_spmd, body=%wide.region_20.22_spmd.sunk | while | flops 342559744 | bytes 17839224 | solution.py:196
  377.1 3.0 fusion.229
  390.6 3.0 fusion.229
  404.1 3.0 fusion.229
  417.6 3.0 fusion.229
  431.1 3.0 fusion.229
  444.6 3.0 fusion.229
  456.6 3.1 convolution_convert_fusion.3
  459.8 6.5 convolution_convert_fusion.2
  467.4 6.7 convolution_convert_fusion.1
  474.2 5.4 reduce-scatter.19.cloned.1.call-done
  481.5 28.4 %reduce-scatter.21.cloned.1.call-done = bf16[192,768]{1,0:T(8,128)(2,1)} async-done(((bf16[768,768]{1,0:T(8,128)(2,1)}), bf16[192,768]{1,0:T(8,128)(2,1)}) %reduce-scatter.21.cloned.1.call-update) | async-done | bytes 294928
  511.8 28.4 %reduce-scatter.23.cloned.1.call-done = bf16[192,768]{1,0:T(8,128)(2,1)} async-done(((bf16[768,768]{1,0:T(8,128)(2,1)}), bf16[192,768]{1,0:T(8,128)(2,1)}) %reduce-scatter.23.cloned.1.call-update) | async-done | bytes 294928
  542.0 28.2 %reduce-scatter.13.cloned.1.call-done = bf16[192,768]{1,0:T(8,128)(2,1)} async-done(((bf16[768,768]{1,0:T(8,128)(2,1)}), bf16[192,768]{1,0:T(8,128)(2,1)}) %reduce-scatter.13.cloned.1.call-update) | async-done | bytes 294928 | tf_op jit(solution)/shard_map/reduce_scatter | solution.py:301
  570.2 86.3 %reduce-scatter.15.cloned.1.call-done = bf16[192,3072]{1,0:T(8,128)(2,1)} async-done(((bf16[768,3072]{1,0:T(8,128)(2,1)}), bf16[192,3072]{1,0:T(8,128)(2,1)}) %reduce-scatter.15.cloned.1.call-update) | async-done | bytes 1179664 | tf_op jit(solution)/shard_map/reduce_scatter | solution.py:304
  656.5 88.0 %reduce-scatter.17.cloned.1.call-done = bf16[768,768]{1,0:T(8,128)(2,1)} async-done(((bf16[3072,768]{1,0:T(8,128)(2,1)}), bf16[768,768]{1,0:T(8,128)(2,1)}) %reduce-scatter.17.cloned.1.call-update) | async-done | bytes 1179664 | tf_op jit(solution)/shard_map/reduce_scatter | solution.py:307
  744.9 42.4 %all-reduce = (f32[768]{0:T(1024)}, f32[768]{0:T(1024)}, f32[768]{0:T(1024)}, f32[3072]{0:T(1024)}, f32[768]{0:T(1024)}, /*index=5*/f32[768]{0:T(1024)}, f32[768]{0:T(1024)}, f32[768]{0:T(1024)}, f32[768]{0:T(1024)}) all-reduce(f32[768]{0:T(1024)S(1)} %bitcast.217, ...), channel_id=1, replica_groups=mesh['rep'=8,'shard'=4] {'rep','shard'}, use_global_device_ids=true, to_apply=%region_36.37 | all-reduce | flops 9216 | bytes 73728 | tf_op jit(solution)/shard_map/psum | solution.py:319
  792.8 36.3 %all-reduce.4.cloned.1.call-done = (bf16[192,768]{0,1:T(8,128)(2,1)}, bf16[192,768]{0,1:T(8,128)(2,1)}, bf16[192,768]{0,1:T(8,128)(2,1)}, bf16[192,768]{1,0:T(8,...) async-done(((bf16[192,768]{0,1:T(8,128)(2,1)}, bf16[192,768]{0,1:T(8,128)(2,1)}, bf16[192,768]{0,1:T(8,128)(2,1)}, bf16[192,768]{1,0:T(8,128)(2,1)}, ...) | async-done | bytes 3538960 | tf_op jit(solution)/shard_map/psum | solution.py:312
  829.0 3.0 convert_element_type.230
  (312 shorter events, 143.2 us)
Async XLA Ops:
  7.2 35.6 %copy-start.32 = (bf16[512,768]{1,0:T(8,128)(2,1)S(1)}, bf16[512,768]{1,0:T(8,128)(2,1)}, u32[]{:S(2)}) copy-start(bf16[512,768]{1,0:T(8,128)(2,1)} %param.23) | copy-start | bytes 2359300
  7.2 35.6 %copy-start.38 = (f32[768]{0:T(1024)S(1)}, f32[768]{0:T(1024)}, u32[]{:S(2)}) copy-start(f32[768]{0:T(1024)} %param.31) | copy-start | bytes 9220
  7.2 35.6 %all-gather.7.cloned.1.call-start = ((), (), s32[]{:S(2)}) async-start(), calls=%async_computation.6 | async-start | bytes 1474560 | tf_op jit(solution)/shard_map/all_gather | solution.py:275
  7.9 66.0 %all-gather.9.cloned.1.call-start = ((), (), s32[]{:S(2)}) async-start(), calls=%async_computation.7 | async-start | bytes 1474560 | tf_op jit(solution)/shard_map/all_gather | solution.py:273
  8.7 96.4 %all-gather.11.cloned.1.call-start = ((), (), s32[]{:S(2)}) async-start(), calls=%async_computation.8 | async-start | bytes 1474560 | tf_op jit(solution)/shard_map/all_gather | solution.py:274
  9.4 128.8 %all-gather.13.cloned.1.call-start = ((), (), s32[]{:S(2)}) async-start(), calls=%async_computation.9 | async-start | bytes 1474560 | tf_op jit(solution)/shard_map/all_gather | solution.py:276
  10.0 216.1 %all-gather.15.cloned.1.call-start = ((), (), s32[]{:S(2)}) async-start(), calls=%async_computation.10 | async-start | bytes 5898240 | tf_op jit(solution)/shard_map/all_gather | solution.py:277
  10.6 304.8 %all-gather.17.cloned.1.call-start = ((), (), s32[]{:S(2)}) async-start(), calls=%async_computation.11 | async-start | bytes 5898240 | tf_op jit(solution)/shard_map/all_gather | solution.py:278
  11.2 468.5 %reduce-scatter.19.cloned.1.call-start = ((), (), s32[]{:S(2)}) async-start(), calls=%async_computation.15 | async-start | bytes 1474560
  11.3 62.7 %copy-start.39 = (f32[768]{0:T(1024)S(1)}, f32[768]{0:T(1024)}, u32[]{:S(2)}) copy-start(f32[768]{0:T(1024)} %param.30) | copy-start | bytes 9220
  122.0 16.2 %copy-start.40 = (f32[768]{0:T(1024)S(1)}, f32[768]{0:T(1024)}, u32[]{:S(2)}) copy-start(f32[768]{0:T(1024)} %param.32) | copy-start | bytes 9220
  138.2 3.6 copy-start.16
  138.2 3.6 copy-start.30
  138.2 3.6 copy-start.33
  141.9 84.3 %copy-start.26 = (f32[768]{0:T(1024)S(1)}, f32[768]{0:T(1024)}, u32[]{:S(2)}) copy-start(f32[768]{0:T(1024)} %param.35) | copy-start | bytes 9220
  141.9 84.3 %copy-start.37 = (f32[3072]{0:T(1024)S(1)}, f32[3072]{0:T(1024)}, u32[]{:S(2)}) copy-start(f32[3072]{0:T(1024)} %param.33) | copy-start | bytes 36868
  141.9 84.2 %copy-start.42 = (f32[768]{0:T(1024)S(1)}, f32[768]{0:T(1024)}, u32[]{:S(2)}) copy-start(f32[768]{0:T(1024)} %param.36) | copy-start | bytes 9220
  144.3 171.1 %copy-start.41 = (f32[768]{0:T(1024)S(1)}, f32[768]{0:T(1024)}, u32[]{:S(2)}) copy-start(f32[768]{0:T(1024)} %param.34) | copy-start | bytes 9220
  322.2 24.9 %copy-start.9 = (bf16[512,768]{1,0:T(8,128)(2,1)S(1)}, bf16[512,768]{1,0:T(8,128)(2,1)}, u32[]{:S(2)}) copy-start(bf16[512,768]{1,0:T(8,128)(2,1)} %param.39) | copy-start | bytes 2359300
  322.2 24.9 %copy-start.24 = (f32[768]{0:T(1024)S(1)}, f32[768]{0:T(1024)}, u32[]{:S(2)}) copy-start(f32[768]{0:T(1024)} %param.37) | copy-start | bytes 9220
  347.8 11.3 %slice-start = ((s8[4718592]{0:T(1024)(128)(4,1)}), s8[4194304]{0:T(1024)(128)(4,1)S(1)}, s32[]{:S(2)}) async-start(s8[4718592]{0:T(1024)(128)(4,1)} %bitcast.219), calls=%async_computation.19 | async-start | bytes 8388608
  349.8 9.3 %copy-start.17 = (bf16[512,768]{1,0:T(8,128)(2,1)}, bf16[512,768]{1,0:T(8,128)(2,1)S(1)}, u32[]{:S(2)}) copy-start(bf16[512,768]{1,0:T(8,128)(2,1)S(1)} %get-tuple-element.245) | copy-start | bytes 2359300
  350.4 8.7 %copy-start.5 = (f32[512,768]{1,0:T(8,128)S(1)}, f32[512,768]{1,0:T(8,128)}, u32[]{:S(2)}) copy-start(f32[512,768]{1,0:T(8,128)} %copy-done.4) | copy-start | bytes 4718596
  350.4 8.7 %slice-start.1 = ((s8[4718592]{0:T(1024)(128)(4,1)}), s8[524288]{0:T(1024)(128)(4,1)S(1)}, s32[]{:S(2)}) async-start(s8[4718592]{0:T(1024)(128)(4,1)} %bitcast.219), calls=%async_computation.20 | async-start | bytes 1048576
  451.9 58.0 %reduce-scatter.21.cloned.1.call-start = ((), (), s32[]{:S(2)}) async-start(), calls=%async_computation.16 | async-start | bytes 1474560
  454.2 85.9 %reduce-scatter.23.cloned.1.call-start = ((), (), s32[]{:S(2)}) async-start(), calls=%async_computation.17 | async-start | bytes 1474560
  456.6 113.7 %reduce-scatter.13.cloned.1.call-start = ((), (), s32[]{:S(2)}) async-start(), calls=%async_computation.12 | async-start | bytes 1474560 | tf_op jit(solution)/shard_map/reduce_scatter | solution.py:301
  459.7 196.8 %reduce-scatter.15.cloned.1.call-start = ((), (), s32[]{:S(2)}) async-start(), calls=%async_computation.13 | async-start | bytes 5898240 | tf_op jit(solution)/shard_map/reduce_scatter | solution.py:304
  466.3 278.2 %reduce-scatter.17.cloned.1.call-start = ((), (), s32[]{:S(2)}) async-start(), calls=%async_computation.14 | async-start | bytes 5898240 | tf_op jit(solution)/shard_map/reduce_scatter | solution.py:307
  474.1 354.9 %all-reduce.4.cloned.1.call-start = ((), (), s32[]{:S(2)}) async-start(), calls=%async_computation.18 | async-start | bytes 7667712 | tf_op jit(solution)/shard_map/psum | solution.py:312
  511.8 232.8 %copy-start.13 = (bf16[6,512,128]{1,2,0:T(8,128)(2,1)S(1)}, bf16[6,512,128]{1,2,0:T(8,128)(2,1)}, u32[]{:S(2)}) copy-start(bf16[6,512,128]{1,2,0:T(8,128)(2,1)} %get-tuple-element.129) | copy-start | bytes 2359300
  744.5 42.8 %copy-start.28 = (bf16[768,768]{1,0:T(8,128)(2,1)S(1)}, bf16[768,768]{1,0:T(8,128)(2,1)}, u32[]{:S(2)}) copy-start(bf16[768,768]{1,0:T(8,128)(2,1)} %all-gather.9.cloned.1.call-done) | copy-start | bytes 3538948
  (27 other events, 55.2 us)
Sparse Core Ops, SparseCore 0:
  9.6 33.1 all-gather.6
  44.4 29.5 all-gather.8
  75.5 29.5 all-gather.10
  106.5 29.5 all-gather.12
  137.6 88.5 all-gather.14
  227.5 87.8 all-gather.16
  452.0 27.6 reduce-scatter.18
  482.0 27.8 reduce-scatter.20
  512.2 27.8 reduce-scatter.22
  542.3 27.8 reduce-scatter.12
  572.5 83.9 reduce-scatter.14
  658.7 85.7 reduce-scatter.16
  749.2 79.7 all-reduce.3
where the time goes:
time: 848 us; the launch traced here: 844 us
  waiting for transfers between devices  544 us (64%)
  matrix products  167 us (20%)
  local copies, waits for them, and re-layouts  56.2 us (7%)
  blocking collectives  42.4 us (5%)
  other arithmetic  17.8 us (2%)
  between operations  14.8 us (2%)
    reduce_scatter x1, waiting for transfers between devices, shards(): lax.psum_scatter(grad_mats[5].astype(jnp.bfloat16), 'shard', scatter_dime...  88 us
    reduce_scatter x1, waiting for transfers between devices, shards(): lax.psum_scatter(grad_mats[4].astype(jnp.bfloat16), 'shard', scatter_dime...  86.3 us
    all_gather x1, waiting for transfers between devices, shards(): lax.all_gather(inner_weight, 'shard', axis=0, tiled=True)  81.8 us
    all_gather x1, waiting for transfers between devices, shards(): lax.all_gather(outer_weight, 'shard', axis=0, tiled=True)  68.4 us
    unnamed x16, waiting for transfers between devices  65.9 us
    dot_general x8, matrix products, project(): return jnp.dot(left, right, preferred_element_type=jnp.float32)  61 us
    psum x1, blocking collectives, shards(): lax.psum((grad_small[0], grad_small[1], grad_small[2], grad_small[3], gra...  42.4 us
    psum x1, waiting for transfers between devices, shards(): lax.psum(row_shards[0].astype(jnp.bfloat16), 'rep').astype(jnp.float32)  36.3 us
  transfers between devices with their start and end apart: 13, of which 12 were waited for; matrix products, arithmetic and copies ran while one was open for 11% of the time, Pallas kernels for 0%

commit v1 on v0

v1 whole, which is shorter than its diff:
```python
from functools import partial

import jax
import jax.numpy as jnp
from jax import lax
from jax.experimental import pallas as pl
from jax.experimental.pallas import tpu as pltpu
from jax.sharding import PartitionSpec as P

HEADS = 12
HD = 64
LEN = 512
D = 768
FF = 3072
EPS = 1e-05
ERF_P = 0.43
ERF_C = (0.2425386708813374, 0.24398923753041435, 0.20746461354880297, 0.2382254793532983, -0.06885152354982843, 0.3647704954681695, -0.29905190193018827, 0.0709147474121678)
F32 = jnp.float32
BF16 = jnp.bfloat16
MESH = pl.DeviceIdType.MESH


def nn(a, b):
    return jnp.dot(a, b, preferred_element_type=F32)


def nt(a, b):
    return lax.dot_general(a, b, (((1,), (1,)), ((), ())), preferred_element_type=F32)


def tn(a, b):
    return lax.dot_general(a, b, (((0,), (0,)), ((), ())), preferred_element_type=F32)


def norm_cdf_pdf(v):
    e = jnp.exp(v * v * (-0.5))
    t = 1.0 / (1.0 + (ERF_P * 0.7071067811865476) * jnp.abs(v))
    poly = jnp.full_like(t, ERF_C[-1])
    for coef in ERF_C[-2::-1]:
        poly = poly * t + coef
    half = (0.5 * t) * poly * e
    return jnp.where(v >= 0, 1.0 - half, half), e * 0.3989422804014327


def fold8(v):
    return jnp.sum(v.reshape(v.shape[0] // 8, 8, v.shape[1]), axis=0)


def whole(w):
    return w[...].reshape(w.shape[0] * w.shape[1], w.shape[2])


class Ctx:
    pass


def ph_qkv(s):
    for w, b, dst in ((s.wq, s.bq, s.q), (s.wk, None, s.k), (s.wv, s.bv, s.v)):
        @pl.loop(0, 3)
        def _(j):
            cols = pl.ds(pl.multiple_of(j * 256, 256), 256)
            r = nn(s.x[...], w[:, :, cols].reshape(D, 256))
            if b is not None:
                r = r + b[:, cols]
            if dst is s.q:
                r = r.astype(BF16).astype(F32) * (HD ** -0.5)
            dst[:, cols] = r.astype(BF16)


def ph_transpose(src, dst, n):
    @pl.loop(0, n // 128)
    def _(j):
        c = pl.ds(pl.multiple_of(j * 128, 128), 128)
        dst[c, :] = src[:, c].T


def ph_untranspose(src, dst, n):
    @pl.loop(0, n // 128)
    def _(j):
        c = pl.ds(pl.multiple_of(j * 128, 128), 128)
        dst[:, c] = src[c, :].T


def head_mask(h):
    lane = lax.broadcasted_iota(jnp.int32, (1, 128), 1)
    return (lane < HD) if h == 0 else (lane >= HD)


def ph_attend(s, lo, hi):
    @pl.loop(lo, hi)
    def _(j):
        c = pl.ds(pl.multiple_of(j * 128, 128), 128)
        kp = s.k[:, c]
        qp = s.q[:, c]
        for h in range(2):
            km = jnp.where(head_mask(h), kp, jnp.zeros_like(kp))
            st = nt(km, qp)
            m = jnp.max(st, axis=0, keepdims=True)
            e = jnp.exp(st - m)
            tot = jnp.sum(e, axis=0, keepdims=True)
            p = (e * (1.0 / tot)).astype(BF16)
            s.probs[2 * j + h] = p
            rows = pl.ds(pl.multiple_of(j * 128 + h * HD, HD), HD)
            s.ctxT[rows, :] = nn(s.vT[rows, :], p).astype(BF16)


def ph_first(s):
    @pl.loop(0, 2)
    def _(i):
        r = pl.ds(pl.multiple_of(i * 256, 256), 256)
        s.acc[r, :] = nn(s.ctx[r, :], whole(s.wo))

    @pl.loop(0, 8)
    def _(i):
        r = pl.ds(pl.multiple_of(i * 64, 64), 64)
        v = s.acc[r, :] + s.x[r, :].astype(F32) + s.bo[...]
        mean = jnp.mean(v, axis=-1, keepdims=True)
        cen = v - mean
        var = jnp.mean(cen * cen, axis=-1, keepdims=True)
        rstd = lax.rsqrt(var + EPS)
        n = cen * rstd
        s.n1[r, :] = n.astype(s.n1.dtype)
        s.r1[r, :] = jnp.broadcast_to(rstd, (64, 128))
        first = n * s.g1[...] + s.b1[...]
        s.fl[r, :] = first.astype(BF16)
        s.acc[r, :] = first + s.b2[...]


def ph_ffn_up(s, lo, hi):
    @pl.loop(lo, hi)
    def _(j):
        c = pl.ds(pl.multiple_of(j * 256, 256), 256)
        s.pre[...] = nn(s.fl[...], s.wi[:, :, c].reshape(D, 256))
        bias = s.bi[:, c]

        @pl.loop(0, 8, unroll=True)
        def _(i):
            r = pl.ds(i * 64, 64)
            v = s.pre[r, :] + bias
            cdf, pdf = norm_cdf_pdf(v)
            s.hid[r, c] = (v * cdf).astype(BF16)
            s.dact[r, c] = (cdf + v * pdf).astype(BF16)


def ph_ffn_down(s):
    rows = s.w2.shape[1]

    @pl.loop(0, FF // rows)
    def _(j):
        c = pl.ds(pl.multiple_of(j * rows, rows), rows)
        s.acc[...] += nn(s.hid[:, c], s.w2[j])


def ph_second(s):
    zero = jnp.zeros((8, D), F32)

    def body(i, carry):
        dg, db, dbo = carry
        r = pl.ds(pl.multiple_of(i * 64, 64), 64)
        v = s.acc[r, :]
        mean = jnp.mean(v, axis=-1, keepdims=True)
        cen = v - mean
        var = jnp.mean(cen * cen, axis=-1, keepdims=True)
        rstd = lax.rsqrt(var + EPS)
        n = cen * rstd
        cot = s.cot[r, :].astype(F32)
        s.out[r, :] = (n * s.g2[...] + s.sh2[...]).astype(BF16)
        cn = cot * n
        gc = cot * s.g2[...]
        m1 = jnp.mean(gc, axis=-1, keepdims=True)
        m2 = jnp.mean(gc * n, axis=-1, keepdims=True)
        g = rstd * (gc - m1 - n * m2)
        s.acc[r, :] = g
        low = g.astype(BF16)
        s.go[r, :] = low
        return dg + fold8(cn), db + fold8(cot), dbo + fold8(low.astype(F32))

    dg, db, dbo = lax.fori_loop(0, 8, body, (zero, zero, zero))
    s.small[6:7, :] = jnp.sum(dg, axis=0, keepdims=True)
    s.small[7:8, :] = jnp.sum(db, axis=0, keepdims=True)
    s.small[3:4, :] = jnp.sum(dbo, axis=0, keepdims=True)


def ph_ffn_back_a(s, lo, hi):
    tile = 256 if s.w2.shape[1] % 256 == 0 else 128
    per = s.w2.shape[1] // tile

    @pl.loop(lo * 256 // tile, hi * 256 // tile)
    def _(j):
        c = pl.ds(pl.multiple_of(j * tile, tile), tile)
        z = j // per
        p = j - z * per
        w = pl.ds(pl.multiple_of(p * tile, tile), tile)
        s.pre[:, :tile] = nt(s.go[...], s.w2[z, w, :])
        s.w2[z, w, :] = tn(s.hid[:, c], s.go[...]).astype(BF16)
        tot = jnp.zeros((8, tile), F32)
        for i in range(8):
            r = pl.ds(i * 64, 64)
            g = (s.pre[r, :tile] * s.dact[r, c].astype(F32)).astype(BF16)
            s.hid[r, c] = g
            tot = tot + fold8(g.astype(F32))
        s.ib[0:1, c] = jnp.sum(tot, axis=0, keepdims=True)


def ph_ffn_back_b(s, lo, hi, step):
    shape = s.wi.shape

    @pl.loop(lo, hi, step=step)
    def _(j):
        c = pl.ds(pl.multiple_of(j * D, D), D)
        s.acc[...] += nt(s.hid[:, c], s.wi[:, :, c].reshape(D, D))
        s.wi[:, :, c] = nn(s.flT[...], s.hid[:, c]).astype(BF16).reshape(shape[0], shape[1], D)


def ph_first_back(s):
    zero = jnp.zeros((8, D), F32)

    def body(i, carry):
        dg, db, dbo = carry
        r = pl.ds(pl.multiple_of(i * 64, 64), 64)
        n = s.n1[r, :].astype(F32)
        rstd = s.r1[r, :][:, 0:1]
        gf = s.acc[r, :]
        gc = gf * s.g1[...]
        m1 = jnp.mean(gc, axis=-1, keepdims=True)
        m2 = jnp.mean(gc * n, axis=-1, keepdims=True)
        g = rstd * (gc - m1 - n * m2)
        s.acc[r, :] = g
        low = g.astype(BF16)
        s.gm[r, :] = low
        return dg + fold8(gf * n), db + fold8(gf), dbo + fold8(low.astype(F32))

    dg, db, dbo = lax.fori_loop(0, 8, body, (zero, zero, zero))
    s.small[4:5, :] = jnp.sum(dg, axis=0, keepdims=True)
    s.small[5:6, :] = jnp.sum(db, axis=0, keepdims=True)
    s.small[2:3, :] = jnp.sum(dbo, axis=0, keepdims=True)


def ph_out_back(s):
    @pl.loop(0, 2)
    def _(i):
        r = pl.ds(pl.multiple_of(i * 256, 256), 256)
        s.gc[r, :] = nt(s.gm[r, :], whole(s.wo)).astype(BF16)
    weight_grad(s.ctxT, s.gm, s.wo)


def ph_attend_back(s, lo, hi):
    @pl.loop(lo, hi)
    def _(j):
        c = pl.ds(pl.multiple_of(j * 128, 128), 128)
        vp = s.v[:, c]
        gp = s.gc[:, c]
        qp = s.q[:, c]
        dk = []
        dv = []
        for h in range(2):
            vm = jnp.where(head_mask(h), vp, jnp.zeros_like(vp))
            p = s.probs[2 * j + h]
            dp = nt(vm, gp)
            pf = p.astype(F32)
            pd = pf * dp
            rd = jnp.sum(pd, axis=0, keepdims=True)
            ds = (pd - pf * rd).astype(BF16)
            rows = pl.ds(pl.multiple_of(j * 128 + h * HD, HD), HD)
            s.dqT[rows, :] = (nn(s.kT[rows, :], ds) * (HD ** -0.5)).astype(BF16)
            dk.append(nn(ds, qp))
            dv.append(nn(p, gp))
        s.dk[:, c] = jnp.where(head_mask(0), dk[0], dk[1]).astype(BF16)
        s.dv[:, c] = jnp.where(head_mask(0), dv[0], dv[1]).astype(BF16)
        s.dq[:, c] = s.dqT[c, :].T


def colsum(src, small, row):
    def body(i, tot):
        r = pl.ds(pl.multiple_of(i * 64, 64), 64)
        return tot + fold8(src[r, :].astype(F32))
    tot = lax.fori_loop(0, 8, body, jnp.zeros((8, D), F32))
    small[row:row + 1, :] = jnp.sum(tot, axis=0, keepdims=True)


def weight_grad(leftT, right, w):
    rows = w.shape[1]

    @pl.loop(0, w.shape[0])
    def _(j):
        w[j] = nn(leftT[pl.ds(pl.multiple_of(j * rows, rows), rows), :], right[...]).astype(BF16)


def ph_in_back(s):
    @pl.loop(0, 2)
    def _(i):
        r = pl.ds(pl.multiple_of(i * 256, 256), 256)
        s.ig[r, :] = s.acc[r, :] + nt(s.dq[r, :], whole(s.wq)) + nt(s.dk[r, :], whole(s.wk)) + nt(s.dv[r, :], whole(s.wv))


class Net:
    def __init__(self, send_sem, recv_sem):
        self.send_sem, self.recv_sem, self.count = send_sem, recv_sem, 0
        rep = lax.axis_index("rep")
        self.z = lax.axis_index("shard")
        self.rep, self.c, self.q = rep, lax.rem(rep, 2), lax.div(rep, 2)
        self.sent = []

    def partner(self):
        return (self.q * 2 + (1 - self.c), self.z)

    def plane(self, d):
        return (lax.bitwise_xor(self.q, d) * 2 + self.c, self.z)

    def line(self, d):
        return (self.rep, lax.rem(self.z + d, 4))

    def push(self, src, dst, dev):
        i = self.count
        self.count += 1
        cp = pltpu.make_async_remote_copy(src_ref=src, dst_ref=dst, send_sem=self.send_sem.at[i], recv_sem=self.recv_sem.at[i],
                                          device_id=dev, device_id_type=MESH)
        cp.start()
        self.sent.append(cp)
        return cp

    def drain(self):
        for cp in self.sent:
            cp.wait_send()
        self.sent = []

    def barrier(self):
        bar = pltpu.get_barrier_semaphore()
        peers = [self.partner()] + [self.plane(d) for d in (1, 2, 3)] + [self.line(d) for d in (1, 2, 3)]
        for dev in peers:
            pl.semaphore_signal(bar, inc=1, device_id=dev, device_id_type=MESH)
        pl.semaphore_wait(bar, len(peers))


def arrived(copies):
    for cp in copies:
        cp.wait_recv()


def span(start, size):
    return pl.ds(pl.multiple_of(start, size), size)


class Gather:
    def __init__(self, net, shard, full, relay):
        self.net, self.shard, self.full, self.relay = net, shard, full, relay
        _, self.rz, n = full.shape
        self.rq, self.nh = self.rz // 4, n // 2
        self.cols = span(net.c * self.nh, self.nh)

    def rows(self, q):
        return span(q * self.rq, self.rq)

    def line(self):
        net = self.net
        r = self.rows(net.q)
        self.a = [net.push(self.shard.at[r, self.cols], self.full.at[net.z, r, self.cols], net.line(d)) for d in (1, 2, 3)]

    def plane(self):
        net = self.net
        arrived(self.a)
        r = self.rows(net.q)
        self.b = []
        for d in (1, 2, 3):
            ref = self.full.at[lax.rem(net.z + d, 4), r, self.cols]
            self.b += [net.push(ref, ref, net.plane(1)), net.push(ref, ref, net.plane(2))]

    def diagonal(self):
        net = self.net
        arrived(self.b)
        self.e = []
        for d in (1, 2, 3):
            zz = lax.rem(net.z + d, 4)
            for via in (1, 2):
                q = lax.bitwise_xor(net.q, 3 - via)
                if self.relay == "rows":
                    h = self.rq // 2
                    ref = self.full.at[zz, span(q * self.rq + (via - 1) * h, h), self.cols]
                elif self.relay == "cols":
                    h = self.nh // 2
                    ref = self.full.at[zz, self.rows(q), span(net.c * self.nh + (via - 1) * h, h)]
                elif self.relay == via:
                    ref = self.full.at[zz, self.rows(q), self.cols]
                else:
                    continue
                self.e.append(net.push(ref, ref, net.plane(via)))

    def share(self):
        net = self.net
        arrived(self.e)
        self.f = []
        for d in (1, 2, 3):
            ref = self.full.at[lax.rem(net.z + d, 4), :, self.cols]
            self.f.append(net.push(ref, ref, net.partner()))

    def done(self):
        arrived(self.f)


class Reduce:
    def __init__(self, net, full, first, part, got, bufs):
        self.net, self.full, self.first, self.second = net, full, first, 3 - first
        _, self.rz, n = full.shape
        self.rq, nh = self.rz // 4, n // 2
        self.nh = nh
        self.pb, self.ab, self.bb, self.zb = bufs
        self.got = got
        kind, k = part
        self.ro, self.rn, self.co, self.cn = 0, self.rq, 0, nh
        if kind == "rows":
            self.rn = self.rq // 2
            self.ro = k * self.rn
        elif kind == "cols":
            self.cn = nh // 2
            self.co = k * self.cn
        self.cols = span(net.c * nh + self.co, self.cn)

    def rows(self, q):
        return span(q * self.rq + self.ro, self.rn)

    def a_send(self):
        net = self.net
        near = lax.bitwise_xor(net.q, self.first)
        far = lax.bitwise_xor(net.q, 3)
        self.a = [net.push(self.full.at[:, self.rows(near), self.cols], self.ab.at[0], net.plane(self.first)),
                  net.push(self.full.at[:, self.rows(far), self.cols], self.ab.at[1], net.plane(self.first))]

    def add(self, q, zs, srcs):
        step = 16

        def body(j, _):
            k = j // (self.rn // step)
            o = (j - k * (self.rn // step)) * step
            r = pl.ds(pl.multiple_of(q * self.rq + self.ro + o, step), step)
            o = pl.ds(pl.multiple_of(o, step), step)
            z = zs if zs is not None else k
            v = self.full[z, r, self.cols].astype(F32)
            for src in srcs:
                v = v + src(k, o).astype(F32)
            self.full[z, r, self.cols] = v.astype(BF16)
            return 0

        lax.fori_loop(0, (1 if zs is not None else 4) * (self.rn // step), body, 0)

    def b_send(self):
        net = self.net
        arrived(self.a)
        mid = lax.bitwise_xor(net.q, self.second)
        self.add(mid, None, [lambda k, o: self.ab[1, k, o, :]])
        self.b = net.push(self.full.at[:, self.rows(mid), self.cols], self.bb, net.plane(self.second))
        self.add(net.q, None, [lambda k, o: self.ab[0, k, o, :]])

    def z_send(self):
        net = self.net
        arrived([self.b])
        self.add(net.q, None, [lambda k, o: self.bb[k, o, :]])
        self.zc = [net.push(self.full.at[lax.rem(net.z + d, 4), self.rows(net.q), self.cols], self.zb.at[d - 1], net.line(d)) for d in (1, 2, 3)]

    def f_send(self, sem):
        net = self.net
        arrived(self.zc)
        self.add(net.q, net.z, [lambda k, o, d=d: self.zb[d, o, :] for d in range(3)])
        src = self.full.at[net.z, self.rows(net.q), self.cols]
        dst = self.got.at[self.rows(net.q), self.cols]
        self.own = pltpu.make_async_copy(src, dst, sem)
        self.own.start()
        self.f = [net.push(src, dst, net.plane(d)) for d in (1, 2, 3)]


class Halves:
    def __init__(self, net, full, pb, part):
        self.net, self.full, self.pb = net, full, pb
        _, self.rz, n = full.shape
        self.nh = n // 2
        self.co, self.cn = 0, self.nh
        if part[0] == "cols":
            self.cn = self.nh // 2
            self.co = part[1] * self.cn

    def send(self):
        net = self.net
        ref = self.full.at[:, :, span((1 - net.c) * self.nh + self.co, self.cn)]
        self.p = net.push(ref, self.pb, net.partner())

    def take(self):
        net = self.net
        arrived([self.p])
        cols = span(net.c * self.nh + self.co, self.cn)
        step = 16
        per = self.rz // step

        def body(j, _):
            k = j // per
            r = pl.ds(pl.multiple_of((j - k * per) * step, step), step)
            self.full[k, r, cols] = (self.full[k, r, cols].astype(F32) + self.pb[k, r, :].astype(F32)).astype(BF16)
            return 0

        lax.fori_loop(0, 4 * per, body, 0)


def back_rows(net, reds):
    for u in reds:
        u.own.wait()
        arrived(u.f)
    got = reds[0].got
    nh = reds[0].nh
    ref = got.at[:, span(net.c * nh, nh)]
    return net.push(ref, ref, net.partner())


def recv_list(shards):
    vm = pltpu.VMEM
    out = {}
    for name, rz, n, parts in (("q", shards[0], D, 1), ("k", shards[0], D, 1), ("v", shards[0], D, 1), ("o", shards[0], D, 1),
                               ("i", shards[0], FF, 2), ("2", shards[1], D, 2)):
        rows = rz if name == "2" else rz
        for u in range(parts):
            cn = n // 2 // (parts if name == "i" else 1)
            rn = rz // 4 // (parts if name == "2" else 1)
            if not (name == "2" and u == 1):
                out["pb%s%d" % (name, u)] = vm((4, rows, cn), BF16)
            out["ab%s%d" % (name, u)] = vm((2, 4, rn, cn), BF16)
            out["bb%s%d" % (name, u)] = vm((4, rn, cn), BF16)
            out["zb%s%d" % (name, u)] = vm((3, rn, cn), BF16)
    out["sp"] = vm((16, D), F32)
    out["sq"] = vm((4, 16, D), F32)
    out["sz"] = vm((4, 16, D), F32)
    out["send"] = pltpu.SemaphoreType.DMA((COPIES,))
    out["recv"] = pltpu.SemaphoreType.DMA((COPIES,))
    return out


COPIES = 256


def scratch_list(shards, comm):
    vm = pltpu.VMEM
    r1, r2 = shards
    n = D // r1
    out = dict(
        wq=vm((n, r1, D), BF16), wk=vm((n, r1, D), BF16), wv=vm((n, r1, D), BF16), wo=vm((n, r1, D), BF16),
        wi=vm((n, r1, FF), BF16), w2=vm((n, r2, D), BF16),
        x=vm((LEN, D), BF16), cot=vm((LEN, D), BF16), xT=vm((D, LEN), BF16),
        q=vm((LEN, D), BF16), k=vm((LEN, D), BF16), v=vm((LEN, D), BF16),
        kT=vm((D, LEN), BF16), vT=vm((D, LEN), BF16),
        probs=vm((HEADS, LEN, LEN), BF16), ctxT=vm((D, LEN), BF16), ctx=vm((LEN, D), BF16),
        acc=vm((LEN, D), F32), n1=vm((LEN, D), F32), r1=vm((LEN, 128), F32),
        fl=vm((LEN, D), BF16), flT=vm((D, LEN), BF16),
        pre=vm((LEN, 256), F32), hid=vm((LEN, FF), BF16), dact=vm((LEN, FF), BF16),
        go=vm((LEN, D), BF16), small=vm((16, D), F32), ib=vm((8, FF), F32),
        sem=pltpu.SemaphoreType.DMA((24,)),
    )
    if comm:
        out.update(recv_list(shards))
    return out


def layer_kernel(names, comm, x_h, wq_h, wk_h, wv_h, wo_h, wi_h, w2_h, bq, bv, bo, bi, b2, g1, b1, g2, sh2, cot_h,
                 out_h, ig_h, dq_h, dk_h, dv_h, do_h, di_h, d2_h, small_out, *scratch):
    s = Ctx()
    for n, r in zip(names, scratch):
        setattr(s, n, r)
    s.bq, s.bv, s.bo, s.bi, s.b2, s.g1, s.b1, s.g2, s.sh2 = bq, bv, bo, bi, b2, g1, b1, g2, sh2
    s.out = s.cot
    s.gm = s.go
    s.gc = s.ctx
    s.dqT = s.vT
    s.dq, s.dk, s.dv = s.q, s.k, s.v
    s.ig = s.acc
    weights = (s.wq, s.wk, s.wv, s.wo, s.wi, s.w2)
    shards = (wq_h, wk_h, wv_h, wo_h, wi_h, w2_h)
    grads = (dq_h, dk_h, dv_h, do_h, di_h, d2_h)
    if comm:
        net = Net(s.send, s.recv)
        net.barrier()
        gq, gk, gv, go, gi, g2w = gs = [Gather(net, a, b, r) for a, b, r in zip(shards, weights, (1, 2, 1, 2, "cols", "rows"))]
        for g in gs:
            g.line()
        dst = [w.at[net.z] for w in weights]
    else:
        dst = list(weights)
    cps = [pltpu.make_async_copy(a, b, s.sem.at[i]) for i, (a, b) in
           enumerate(zip((x_h, *shards, cot_h), (s.x, *dst, s.cot)))]
    for c in cps:
        c.start()
    s.small[...] = jnp.zeros_like(s.small)
    cps[0].wait()
    ph_transpose(s.x, s.xT, D)
    if comm:
        for g in (gq, gk, gv, go):
            g.plane()
        for g in (gq, gk, gv, go):
            g.diagonal()
        for g in (gq, gk, gv):
            g.share()
        for g in (gq, gk, gv):
            g.done()
    for i in (1, 2, 3):
        cps[i].wait()
    ph_qkv(s)
    ph_transpose(s.k, s.kT, D)
    ph_transpose(s.v, s.vT, D)
    if comm:
        gi.plane()
        go.share()
        ph_attend(s, 0, 2)
        gi.diagonal()
        ph_attend(s, 2, 4)
        g2w.plane()
        ph_attend(s, 4, 6)
        gi.share()
        go.done()
    else:
        ph_attend(s, 0, 6)
    ph_untranspose(s.ctxT, s.ctx, D)
    cps[4].wait()
    ph_first(s)
    ph_transpose(s.fl, s.flT, D)
    cps[5].wait()
    cps[6].wait()
    if comm:
        gi.done()
        ph_ffn_up(s, 0, 6)
        g2w.diagonal()
        ph_ffn_up(s, 6, 12)
        g2w.share()
        g2w.done()
        net.drain()
    else:
        ph_ffn_up(s, 0, 12)
    ph_ffn_down(s)
    cps[7].wait()
    ph_second(s)
    ocp = pltpu.make_async_copy(s.out, out_h, s.sem.at[0])
    ocp.start()
    ph_ffn_back_a(s, 0, 12)
    for i in range(4):
        s.small[8 + i:9 + i, :] = s.ib[0:1, i * D:(i + 1) * D]
    if not comm:
        ph_ffn_back_b(s, 0, 4, 1)
        ph_first_back(s)
        ph_out_back(s)
        ph_attend_back(s, 0, 6)
        ph_in_back(s)
        icp = pltpu.make_async_copy(s.ig, ig_h, s.sem.at[1])
        icp.start()
        weight_grad(s.xT, s.dq, s.wq)
        weight_grad(s.xT, s.dk, s.wk)
        weight_grad(s.xT, s.dv, s.wv)
        colsum(s.dq, s.small, 0)
        colsum(s.dv, s.small, 1)
        cps = [pltpu.make_async_copy(a, b, s.sem.at[i + 2]) for i, (a, b) in enumerate(zip(weights, grads))]
        for c in cps:
            c.start()
        small_out[...] = s.small[...]
        for c in (ocp, icp, *cps):
            c.wait()
        return

    def unit(w, first, part, got, name):
        return Reduce(net, w, first, part, got, [getattr(s, b + name, None) for b in ("pb", "ab", "bb", "zb")])

    one = ("all", 0)
    u20, u21 = unit(s.w2, 1, ("rows", 0), d2_h, "20"), unit(s.w2, 2, ("rows", 1), d2_h, "21")
    ui0, ui1 = unit(s.wi, 1, ("cols", 0), di_h, "i0"), unit(s.wi, 2, ("cols", 1), di_h, "i1")
    uo, uq, uk, uv = (unit(s.wo, 1, one, do_h, "o0"), unit(s.wq, 2, one, dq_h, "q0"),
                      unit(s.wk, 1, one, dk_h, "k0"), unit(s.wv, 2, one, dv_h, "v0"))
    h2, hi0, hi1 = Halves(net, s.w2, s.pb20, one), Halves(net, s.wi, s.pbi0, ("cols", 0)), Halves(net, s.wi, s.pbi1, ("cols", 1))
    ho, hq, hk, hv = (Halves(net, s.wo, s.pbo0, one), Halves(net, s.wq, s.pbq0, one), Halves(net, s.wk, s.pbk0, one),
                      Halves(net, s.wv, s.pbv0, one))
    h2.send()
    ph_ffn_back_b(s, 0, 4, 2)
    hi0.send()
    h2.take()
    u20.a_send()
    u21.a_send()
    ph_ffn_back_b(s, 1, 4, 2)
    hi1.send()
    hi0.take()
    ui0.a_send()
    ph_first_back(s)
    hi1.take()
    ui1.a_send()
    ph_out_back(s)
    ho.send()
    u20.b_send()
    u21.b_send()
    ph_attend_back(s, 0, 2)
    ho.take()
    uo.a_send()
    ui0.b_send()
    ph_attend_back(s, 2, 4)
    ui1.b_send()
    u20.z_send()
    u21.z_send()
    ph_attend_back(s, 4, 6)
    uo.b_send()
    weights_grad = ((s.dq, s.wq, hq), (s.dk, s.wk, hk), (s.dv, s.wv, hv))
    ph_in_back(s)
    icp = pltpu.make_async_copy(s.ig, ig_h, s.sem.at[1])
    icp.start()
    for d, w, h in weights_grad:
        weight_grad(s.xT, d, w)
        h.send()
    colsum(s.dq, s.small, 0)
    colsum(s.dv, s.small, 1)
    sp = net.push(s.small, s.sp, net.partner())
    for h, u in ((hq, uq), (hk, uk), (hv, uv)):
        h.take()
        u.a_send()
    ui0.z_send()
    ui1.z_send()
    arrived([sp])
    s.sq[net.q] = s.small[...] + s.sp[...]
    sq = [net.push(s.sq.at[net.q], s.sq.at[net.q], net.plane(d)) for d in (1, 2, 3)]
    u20.f_send(s.sem.at[8])
    u21.f_send(s.sem.at[9])
    uo.z_send()
    for u in (uq, uk, uv):
        u.b_send()
    arrived(sq)
    s.sz[net.z] = s.sq[0] + s.sq[1] + s.sq[2] + s.sq[3]
    sz = [net.push(s.sz.at[net.z], s.sz.at[net.z], net.line(d)) for d in (1, 2, 3)]
    ui0.f_send(s.sem.at[10])
    ui1.f_send(s.sem.at[11])
    for u in (uq, uk, uv):
        u.z_send()
    uo.f_send(s.sem.at[12])
    last = [back_rows(net, (u20, u21)), back_rows(net, (ui0, ui1))]
    for i, u in enumerate((uq, uk, uv)):
        u.f_send(s.sem.at[13 + i])
    arrived(sz)
    small_out[...] = s.sz[0] + s.sz[1] + s.sz[2] + s.sz[3]
    last.append(back_rows(net, (uo,)))
    for u in (uq, uk, uv):
        last.append(back_rows(net, (u,)))
    arrived(last)
    net.drain()
    ocp.wait()
    icp.wait()


def layer_call(args, comm):
    x, wq, wk, wv, wo, wi, w2, bq, bv, bo, bi, b2, g1, b1, g2, sh2, cot = args
    rows = [v.reshape(1, -1) for v in (bq, bv, bo, bi, b2, g1, b1, g2, sh2)]
    any_ = pl.BlockSpec(memory_space=pl.ANY)
    vmem = pl.BlockSpec(memory_space=pltpu.VMEM)
    sds = jax.ShapeDtypeStruct
    mats = (wq, wk, wv, wo, wi, w2)
    r1, r2 = wq.shape[-2], w2.shape[-2]
    sc = scratch_list((r1, r2), comm)
    params = dict(collective_id=0, has_side_effects=True) if comm else {}
    return pl.pallas_call(
        partial(layer_kernel, tuple(sc), comm),
        out_shape=(sds((LEN, D), BF16), sds((LEN, D), F32), *(sds(w.shape, BF16) for w in mats), sds((16, D), F32)),
        in_specs=[any_] * 7 + [vmem] * 9 + [any_],
        out_specs=(any_,) * 8 + (vmem,),
        scratch_shapes=list(sc.values()),
        compiler_params=pltpu.CompilerParams(vmem_limit_bytes=67043328, **params),
        cost_estimate=pl.CostEstimate(flops=25 * 10 ** 9, bytes_accessed=40 * 10 ** 6, transcendentals=8 * 10 ** 6),
        name="layer",
    )(x, *mats, *rows, cot)


def shards(rep, line, *args):
    x, mats, vecs, cot = args[0], args[1:7], args[7:16], args[16]
    if (rep, line) == (8, 4):
        res = layer_call((x, *mats, *vecs, cot), True)
        grads = [g.astype(F32) for g in res[2:8]]
        small = res[8]
    else:
        full = [lax.all_gather(w, "shard", axis=0) for w in mats]
        res = layer_call((x, *full, *vecs, cot), False)
        grads = [lax.psum(lax.psum_scatter(g, "shard", scatter_dimension=0), "rep").astype(F32) for g in res[2:8]]
        small = lax.psum(res[8], ("rep", "shard"))
    vec = [small[0], small[1], small[2], small[8:12].reshape(FF), small[3], small[4], small[5], small[6], small[7]]
    return (res[0], res[1], *grads, *vec)


def solution(mesh):
    tok = P(("rep", "shard"), None)
    row = P("shard", None)
    return jax.shard_map(
        partial(shards, mesh.shape["rep"], mesh.shape["shard"]),
        mesh=mesh,
        in_specs=(tok,) + (row,) * 6 + (P(),) * 9 + (tok,),
        out_specs=(tok, tok) + (row,) * 6 + (P(),) * 9,
        check_vma=False,
    )
```

time: 848 us -> 221 us (0.26)
  waiting for transfers between devices: 544 us -> 0 us
  Pallas kernels: 0 us -> 196 us
  matrix products: 167 us -> 0 us
  blocking collectives: 42.4 us -> 0 us
  local copies, waits for them, and re-layouts: 56.2 us -> 15.2 us
  between operations: 14.8 us -> 0.68 us
  other arithmetic: 17.8 us -> 8.02 us
    all_gather x6 -> x0, waiting for transfers between devices: 239 us -> none  [the longest x1 81.8 us: shards(): lax.all_gather(inner_weight, 'shard', axis=0, tiled=True)]
    reduce_scatter x3 -> x0, waiting for transfers between devices: 203 us -> none  [the longest x1 88 us: shards(): lax.psum_scatter(grad_mats[5].astype(jnp.bfloat16), 'shard', scatter_dime...]
    pallas_call x0 -> x1, Pallas kernels: none -> 196 us  [layer_call(): pl.pallas_call(partial(layer_kernel, tuple(sc), comm), out_shape=(sds((LE...]
    dot_general x68 -> x0, matrix products: 162 us -> none  [the longest x8 61 us: project(): return jnp.dot(left, right, preferred_element_type=jnp.float32)]
    unnamed x16 -> x0, waiting for transfers between devices: 65.9 us -> none
    psum x1 -> x0, blocking collectives: 42.4 us -> none  [shards(): lax.psum((grad_small[0], grad_small[1], grad_small[2], grad_small[3], gra...]
    psum x1 -> x0, waiting for transfers between devices: 36.3 us -> none  [shards(): lax.psum(row_shards[0].astype(jnp.bfloat16), 'rep').astype(jnp.float32)]
    unnamed x101 -> x16, local copies, waits for them, and re-layouts: 19.5 us -> 2.05 us
  transfers between devices with their start and end apart: 13 -> 0, of which waited for: 12 -> 0; matrix products, arithmetic and copies ran while one was open for 11% -> 0% of each run, Pallas kernels for 0% -> 0%
where the time goes in v1:
time: 221 us; the launch traced here: 220 us
  Pallas kernels  196 us (89%)
  local copies, waits for them, and re-layouts  15.2 us (7%)
  other arithmetic  8.02 us (4%)
    pallas_call x1, Pallas kernels, layer_call(): pl.pallas_call(partial(layer_kernel, tuple(sc), comm), out_shape=(sds((LE...  196 us
    reshape x8, local copies, waits for them, and re-layouts, layer_call(): rows = [v.reshape(1, -1) for v in (bq, bv, bo, bi, b2, g1, b1, g2, sh2)]  10.1 us
    convert_element_type x6, other arithmetic, shards(): grads = [g.astype(F32) for g in res[2:8]]  8.02 us

profile of v1, /device:TPU:0, one launch (start us, length us, event | category | flops | bytes accessed | tf_op | source)
XLA Modules:
  0.0 219.6 jit_solution(10973579918522666841)
XLA Ops:
  0.7 1.3 reshape.64.bq
  1.9 1.3 reshape.65.bv
  3.2 1.3 reshape.66.bo
  4.5 1.3 reshape.68.b2
  5.7 1.3 reshape.69.g1
  7.0 1.3 reshape.70.b1
  8.3 1.3 reshape.71.g2
  9.5 1.3 reshape.72.sh2
  10.8 195.6 %layer.1 = (bf16[512,768]{1,0:T(8,128)(2,1)}, f32[512,768]{1,0:T(8,128)}, bf16[192,768]{1,0:T(8,128)(2,1)}, bf16[192,768]{1,0:T(8,128)(2,1)}, bf16[192,768]{1,0:...) custom-call(bf16[512,768]{1,0:T(8,128)(2,1)} %x_h.1, ...), custom_call_target="tpu_custom_call" | custom-call | flops 24999999488 | bytes 40000000 | tf_op jit(solution)/shard_map/layer/pallas_call | solution.py:753
  206.4 1.7 slice_reduce_fusion
  208.1 0.7 slice.30
  208.9 0.6 reshape.73
  209.5 0.0 copy-start.1
  209.5 3.0 %convert_element_type.22 = f32[192,3072]{1,0:T(8,128)} convert(bf16[192,3072]{1,0:T(8,128)(2,1)} %get-tuple-element.32) | non-fusion elementwise | flops 589824 | bytes 3538944 | tf_op jit(solution)/shard_map/convert_element_type | solution.py:769
  212.5 0.0 copy-done.1
  212.5 0.0 copy-start.5
  212.5 1.6 convert_element_type.23
  214.1 0.0 copy-start.4
  214.1 0.0 copy-start.3
  214.1 0.0 copy-done.6
  214.1 0.0 copy-start.2
  214.1 0.9 convert_element_type.18
  215.0 0.0 copy-done.5
  215.0 0.9 convert_element_type.19
  215.8 0.0 copy-done.4
  215.8 0.9 convert_element_type.20
  216.7 0.0 copy-done.3
  216.7 0.9 convert_element_type.21
  217.6 0.0 copy-done.2
  217.6 0.9 copy.36
  218.4 0.0 copy-done
  218.4 1.1 copy.37
  (2 shorter events, 0.0 us)
Async XLA Ops:
  209.5 3.0 %copy-start.1 = (bf16[768,768]{1,0:T(8,128)(2,1)S(1)}, bf16[768,768]{1,0:T(8,128)(2,1)}, u32[]{:S(2)}) copy-start(bf16[768,768]{1,0:T(8,128)(2,1)} %get-tuple-element.33) | copy-start | bytes 3538948
  212.5 1.6 copy-start.6
  212.5 2.4 %copy-start.5 = (bf16[192,768]{1,0:T(8,128)(2,1)S(1)}, bf16[192,768]{1,0:T(8,128)(2,1)}, u32[]{:S(2)}) copy-start(bf16[192,768]{1,0:T(8,128)(2,1)} %get-tuple-element.29) | copy-start | bytes 884740
  214.1 1.7 copy-start.4
  214.1 2.6 %copy-start.3 = (bf16[192,768]{1,0:T(8,128)(2,1)S(1)}, bf16[192,768]{1,0:T(8,128)(2,1)}, u32[]{:S(2)}) copy-start(bf16[192,768]{1,0:T(8,128)(2,1)} %get-tuple-element.31) | copy-start | bytes 884740
  214.1 3.4 %copy-start.2 = (bf16[512,768]{1,0:T(8,128)(2,1)S(1)}, bf16[512,768]{1,0:T(8,128)(2,1)}, u32[]{:S(2)}) copy-start(bf16[512,768]{1,0:T(8,128)(2,1)} %get-tuple-element.60) | copy-start | bytes 2359300
  215.8 2.6 %copy-start = (f32[512,768]{1,0:T(8,128)S(1)}, f32[512,768]{1,0:T(8,128)}, u32[]{:S(2)}) copy-start(f32[512,768]{1,0:T(8,128)} %get-tuple-element.61) | copy-start | bytes 4718596
